TPU v7x, 128 devices: a whole 4x4x4 slice. The times are simulated.
128 devices in a mesh: row: 16 (over y, z_hi, core), col: 8 (over x, z_lo).
Axes of the slice: x: 4, y: 4, z: 4 (z_hi: 2, z_lo: 2; z = z_hi * 2 + z_lo), core: 2. Of those that a mesh axis runs over, the one named last changes fastest.
Arguments:
- tokens: bfloat16 [6144, 4096], P('row', 'col'), may hold values from -6 to 6
- cotangent: bfloat16 [6144, 4096], P('row', 'col'), may hold values from -6 to 6
- gate_blocks: bfloat16 [32, 32, 128, 128], P('row', 'col'), may hold values from -0.1875 to 0.1875
- up_blocks: bfloat16 [32, 32, 128, 128], P('row', 'col'), may hold values from -0.1875 to 0.1875
- down_blocks: bfloat16 [32, 32, 128, 128], P('row', 'col'), may hold values from -0.09375 to 0.09375
- gate_cols: int32 [32, 32], P('row', 'col'), may hold values from 0 to 127, as said below
- up_cols: int32 [32, 32], P('row', 'col'), may hold values from 0 to 127, as said below
- down_cols: int32 [32, 32], P('row', 'col'), may hold values from 0 to 127, as said below
Outputs:
- output: bfloat16 [6144, 4096], P('row', 'col')
- tokens_grad: bfloat16 [6144, 4096], P('row', 'col')
- gate_grad: bfloat16 [32, 32, 128, 128], P('row', 'col')
- up_grad: bfloat16 [32, 32, 128, 128], P('row', 'col')
- down_grad: bfloat16 [32, 32, 128, 128], P('row', 'col')
Inputs may be any that keep to these rules, and one draw needn't show every extreme that they name: In every block row of gate_cols, slots c * 4 to c * 4 + 3 hold 4 different block columns, all in c * 16 to c * 16 + 15. In every block row of up_cols, slots c * 4 to c * 4 + 3 hold 4 different block columns, all in c * 16 to c * 16 + 15. In every block row of down_cols, slots c * 4 to c * 4 + 3 hold 4 different block columns, all in c * 16 to c * 16 + 15.
All inputs are finite; a program needn't handle non-finite values.
Results may differ from a plain program's by a relative error of at most 0.022.
Values may be sent and summed in bfloat16 or wider, within the bound.
No kernel may reach another device: no remote copies, remote signals or barrier semaphores. Data moves between devices by JAX's collectives and lax.ppermute only.
A program may use at most 256 MiB of HBM per device.

v0:
```python
import jax
import jax.numpy as jnp
from jax import lax
from jax.sharding import PartitionSpec as P


def spread_columns(products, columns, local_width):
    tok_rows = products.shape[0]
    flat = products.reshape(tok_rows, -1, products.shape[3])
    empty = jnp.zeros((tok_rows, local_width, products.shape[3]), jnp.float32)
    return empty.at[:, columns.reshape(-1)].add(flat)


def body(tokens, cotangent, gate_blocks, up_blocks, down_blocks, gate_cols, up_cols, down_cols):
    local_rows = gate_blocks.shape[0]
    local_slots = gate_blocks.shape[1]
    block_size = gate_blocks.shape[2]
    local_width = 4 * local_slots
    offset = lax.axis_index("col") * local_width
    tok_rows = tokens.shape[0]
    features, cot_features = (
        lax.all_gather(tokens, "col", axis=1, tiled=True),
        lax.all_gather(cotangent, "col", axis=1, tiled=True),
    )
    blocks_all = features.shape[1] // block_size
    feature_blocks = features.reshape(tok_rows, blocks_all, block_size)
    cotangent_blocks = cot_features.reshape(tok_rows, blocks_all, block_size)
    gate_vals = lax.all_gather(gate_blocks, "row", axis=0, tiled=True)
    up_vals = lax.all_gather(up_blocks, "row", axis=0, tiled=True)
    gate_piece = lax.all_gather(gate_cols.astype(jnp.bfloat16), "row", axis=0, tiled=True)
    up_piece = lax.all_gather(up_cols.astype(jnp.bfloat16), "row", axis=0, tiled=True)
    inputs = feature_blocks
    gate_local = gate_piece.astype(jnp.int32) - offset
    up_local = up_piece.astype(jnp.int32) - offset
    gate_products = jnp.einsum(
        "tkd,kjde->tkje", inputs, gate_vals, preferred_element_type=jnp.float32
    )
    up_products = jnp.einsum("tkd,kjde->tkje", inputs, up_vals, preferred_element_type=jnp.float32)
    gate_acc = spread_columns(gate_products, gate_local, local_width)
    up_acc = spread_columns(up_products, up_local, local_width)
    gate_gate_idx = gate_local
    gate_up_idx = up_local
    gate_acc, up_acc, gate_idx, up_idx = (gate_acc, up_acc, gate_gate_idx, gate_up_idx)
    silu_gate = jax.nn.silu(gate_acc)
    hidden_blocks = (silu_gate * up_acc).astype(jnp.bfloat16)
    down_vals = lax.all_gather(down_blocks, "row", axis=0, tiled=True)
    down_piece = lax.all_gather(down_cols.astype(jnp.bfloat16), "row", axis=0, tiled=True)
    down_local = down_piece.astype(jnp.int32) - offset
    chosen = jnp.take(hidden_blocks, down_local, axis=1)
    partial_value = jnp.einsum(
        "tkje,kjde->tkd", chosen, down_vals, preferred_element_type=jnp.float32
    )
    out_acc = partial_value
    down_down_idx = down_local
    out_acc, down_idx = (out_acc, down_down_idx)
    output = lax.psum_scatter(
        out_acc.reshape(tok_rows, -1).astype(jnp.bfloat16), "col", scatter_dimension=1, tiled=True
    )
    inputs = cotangent_blocks
    products = jnp.einsum(
        "tkd,kjde->tkje",
        inputs,
        lax.all_gather(down_blocks, "row", axis=0, tiled=True),
        preferred_element_type=jnp.float32,
    )
    hidden_grad = spread_columns(products, down_idx, local_width)
    sigmoid_gate = jax.nn.sigmoid(gate_acc)
    up_delta = (hidden_grad * silu_gate).astype(jnp.bfloat16)
    gate_delta = (
        hidden_grad * up_acc * sigmoid_gate * (1.0 + gate_acc * (1.0 - sigmoid_gate))
    ).astype(jnp.bfloat16)
    gate_vals = lax.all_gather(gate_blocks, "row", axis=0, tiled=True)
    up_vals = lax.all_gather(up_blocks, "row", axis=0, tiled=True)
    gate_local = gate_idx
    up_local = up_idx
    partial_value = jnp.einsum(
        "tkje,kjde->tkd",
        jnp.take(gate_delta, gate_local, axis=1),
        gate_vals,
        preferred_element_type=jnp.float32,
    )
    partial_value = partial_value + jnp.einsum(
        "tkje,kjde->tkd",
        jnp.take(up_delta, up_local, axis=1),
        up_vals,
        preferred_element_type=jnp.float32,
    )
    tokens_grad = lax.psum_scatter(
        partial_value.reshape(tok_rows, -1).astype(jnp.bfloat16),
        "col",
        scatter_dimension=1,
        tiled=True,
    )
    grad_scale = float(tok_rows * lax.axis_size("row")) ** (-0.5)
    groups = local_rows * lax.axis_size("row") // local_rows

    def one_group(group_index):
        group_first = group_index * local_rows
        inputs = lax.dynamic_slice_in_dim(feature_blocks, group_first, local_rows, 1)
        cot_inputs = lax.dynamic_slice_in_dim(cotangent_blocks, group_first, local_rows, 1)
        gate_local = lax.dynamic_slice_in_dim(gate_idx, group_first, local_rows, 0)
        up_local = lax.dynamic_slice_in_dim(up_idx, group_first, local_rows, 0)
        down_local = lax.dynamic_slice_in_dim(down_idx, group_first, local_rows, 0)
        gate_term = jnp.einsum(
            "tkd,tkje->kjde",
            inputs,
            jnp.take(gate_delta, gate_local, axis=1),
            preferred_element_type=jnp.float32,
        )
        up_term = jnp.einsum(
            "tkd,tkje->kjde",
            inputs,
            jnp.take(up_delta, up_local, axis=1),
            preferred_element_type=jnp.float32,
        )
        down_term = jnp.einsum(
            "tkd,tkje->kjde",
            cot_inputs,
            jnp.take(hidden_blocks, down_local, axis=1),
            preferred_element_type=jnp.float32,
        )
        return jnp.stack([gate_term, up_term, down_term], axis=1) * grad_scale

    stacked = lax.map(one_group, jnp.arange(groups, dtype=jnp.int32))
    weight_grads = lax.psum_scatter(
        stacked.reshape((local_rows * lax.axis_size("row"),) + stacked.shape[2:]).astype(
            jnp.bfloat16
        ),
        "row",
        scatter_dimension=0,
        tiled=True,
    ).astype(jnp.float32)
    gate_grad = weight_grads[:, 0].astype(jnp.bfloat16)
    up_grad = weight_grads[:, 1].astype(jnp.bfloat16)
    down_grad = weight_grads[:, 2].astype(jnp.bfloat16)
    return (output, tokens_grad, gate_grad, up_grad, down_grad)


def solution(mesh):
    in_specs = (
        P("row", "col"),
        P("row", "col"),
        P("row", "col", None, None),
        P("row", "col", None, None),
        P("row", "col", None, None),
        P("row", "col"),
        P("row", "col"),
        P("row", "col"),
    )
    out_specs = (
        P("row", "col"),
        P("row", "col"),
        P("row", "col", None, None),
        P("row", "col", None, None),
        P("row", "col", None, None),
    )
    return jax.shard_map(body, mesh=mesh, in_specs=in_specs, out_specs=out_specs, check_vma=False)
```

profile of v0, /device:TPU:2, one launch (start us, length us, event | category | flops | bytes accessed | tf_op | source)
XLA Modules:
  0.0 1250.2 jit_solution(13534747205828137103)
XLA Ops:
  14.0 28.0 %all-gather = bf16[16,2,4]{2,1,0:T(2,128)(2,1)S(1)} all-gather(bf16[1,2,4]{2,1,0:T(2,128)(2,1)S(1)} %convert_bitcast_fusion.2), channel_id=1, replica_groups=mesh['row'=16,'col'=8] {'row'}, dimensions={0}, use_global_device_ids=true | all-gather | bytes 272 | tf_op jit(solution)/shard_map/all_gather | solution.py:30
  42.8 19.2 %all-gather.1 = bf16[16,2,4]{2,1,0:T(2,128)(2,1)S(1)} all-gather(bf16[1,2,4]{2,1,0:T(2,128)(2,1)S(1)} %convert_bitcast_fusion.1), channel_id=1, replica_groups=mesh['row'=16,'col'=8] {'row'}, dimensions={0}, use_global_device_ids=true | all-gather | bytes 272 | tf_op jit(solution)/shard_map/all_gather | solution.py:31
  62.8 24.5 %all-gather.2 = bf16[16,2,4]{2,1,0:T(2,128)(2,1)S(1)} all-gather(bf16[1,2,4]{2,1,0:T(2,128)(2,1)S(1)} %convert_bitcast_fusion), channel_id=1, replica_groups=mesh['row'=16,'col'=8] {'row'}, dimensions={0}, use_global_device_ids=true | all-gather | bytes 272 | tf_op jit(solution)/shard_map/all_gather | solution.py:47
  87.4 55.0 %all-gather.9.cloned.1.call-done = bf16[32,4,128,128]{3,2,1,0:T(8,128)(2,1)} async-done(((bf16[2,4,128,128]{3,2,1,0:T(8,128)(2,1)}), bf16[32,4,128,128]{3,2,1,0:T(8,128)(2,1)}) %all-gather.9.cloned.1.call-update) | async-done | bytes 4194320 | tf_op jit(solution)/shard_map/all_gather | solution.py:28
  142.5 15.2 %fusion.52 = f32[32,4,128,384]{3,2,1,0:T(8,128)} fusion(bf16[32,4,128,128]{3,2,1,0:T(8,128)(2,1)} %all-gather.9.cloned.1.call-done, bf16[384,32,128,1]{0,2,3,1:T(8,128)(2,1)} %bitcast.176), kind=kOutput, calls=%fused_computation.100 | convolution fusion | flops 1610612736 | bytes 32505856 | tf_op jit(solution)/shard_map/tkd,kjde->tkje/dot_general | solution.py:35
  157.7 25.0 %copy.57 = f32[384,128,128]{2,0,1:T(8,128)} copy(f32[384,128,128]{0,2,1:T(8,128)} %bitcast.166) | data formatting | bytes 50331648 | tf_op jit(solution)/shard_map/reshape | solution.py:9
  182.7 16.9 %all-gather.13.cloned.1.call-done = bf16[32,4,128,128]{3,2,1,0:T(8,128)(2,1)} async-done(((bf16[2,4,128,128]{3,2,1,0:T(8,128)(2,1)}), bf16[32,4,128,128]{3,2,1,0:T(8,128)(2,1)}) %all-gather.13.cloned.1.call-update) | async-done | bytes 4194320 | tf_op jit(solution)/shard_map/all_gather | solution.py:29
  199.6 14.1 %fusion.53 = f32[32,4,128,384]{3,2,1,0:T(8,128)} fusion(bf16[32,4,128,128]{3,2,1,0:T(8,128)(2,1)} %all-gather.13.cloned.1.call-done, bf16[384,32,128,1]{0,2,3,1:T(8,128)(2,1)S(1)} %bitcast.178), kind=kOutput, calls=%fused_computation.101 | convolution fusion | flops 1610612736 | bytes 32505856 | tf_op jit(solution)/shard_map/tkd,kjde->tkje/dot_general | solution.py:38
  213.7 24.8 %copy.60 = f32[384,128,128]{2,0,1:T(8,128)} copy(f32[384,128,128]{0,2,1:T(8,128)} %bitcast.167) | data formatting | bytes 50331648 | tf_op jit(solution)/shard_map/reshape | solution.py:9
  238.5 32.8 %all-gather.17.cloned.1.call-done = bf16[384,4096]{0,1:T(8,128)(2,1)} async-done(((bf16[384,512]{0,1:T(8,128)(2,1)}), bf16[384,4096]{0,1:T(8,128)(2,1)}) %all-gather.17.cloned.1.call-update) | async-done | bytes 3145744 | tf_op jit(solution)/shard_map/all_gather | solution.py:23
  271.3 58.6 %all-gather.15.cloned.1.call-done = bf16[32,4,128,128]{3,2,1,0:T(8,128)(2,1)} async-done(((bf16[2,4,128,128]{3,2,1,0:T(8,128)(2,1)}), bf16[32,4,128,128]{3,2,1,0:T(8,128)(2,1)}) %all-gather.15.cloned.1.call-update) | async-done | bytes 4194320 | tf_op jit(solution)/shard_map/all_gather | solution.py:46
  329.9 14.9 %fusion.54 = f32[32,4,128,384]{3,2,1,0:T(8,128)} fusion(bf16[32,4,128,128]{3,2,1,0:T(8,128)(2,1)} %all-gather.15.cloned.1.call-done, bf16[384,32,128,1]{0,2,3,1:T(8,128)(2,1)} %bitcast.182), kind=kOutput, calls=%fused_computation.102 | convolution fusion | flops 1610612736 | bytes 32505856 | tf_op jit(solution)/shard_map/tkd,kjde->tkje/dot_general | solution.py:60
  344.9 24.7 %copy.65 = f32[384,128,128]{2,0,1:T(8,128)} copy(f32[384,128,128]{0,2,1:T(8,128)} %bitcast.168) | data formatting | bytes 50331648 | tf_op jit(solution)/shard_map/reshape | solution.py:9
  369.8 38.7 %scatter_fusion = f32[384,16,128]{2,0,1:T(8,128)S(1)} fusion(f32[384,16,128]{2,0,1:T(8,128)S(1)} %broadcast.80.clone, s32[128]{0:T(128)S(1)} %fusion.46, f32[128,384,128]{2,1,0:T(8,128)} %bitcast.169), kind=kCustom, calls=%fused_computation.6 | custom fusion | flops 6291456 | bytes 75497984 | tf_op jit(solution)/shard_map/scatter-add | solution.py:11
  410.8 63.0 %scatter_fusion.1 = f32[384,16,128]{2,0,1:T(8,128)} fusion(f32[384,16,128]{2,0,1:T(8,128)} %broadcast.80.clone.2, s32[128]{0:T(128)S(1)} %fusion.47, f32[128,384,128]{2,1,0:T(8,128)} %bitcast.170), kind=kCustom, calls=%fused_computation.7 | custom fusion | flops 6291456 | bytes 75497984 | tf_op jit(solution)/shard_map/scatter-add | solution.py:11
  474.2 38.7 %scatter_fusion.2 = f32[384,16,128]{2,0,1:T(8,128)S(1)} fusion(f32[384,16,128]{2,0,1:T(8,128)S(1)} %broadcast.80.clone.1, s32[128]{0:T(128)S(1)} %fusion.48, f32[128,384,128]{2,1,0:T(8,128)} %bitcast.171), kind=kCustom, calls=%fused_computation.8 | custom fusion | flops 6291456 | bytes 75497984 | tf_op jit(solution)/shard_map/scatter-add | solution.py:11
  512.9 5.7 multiply_convert_fusion.1
  518.7 278.2 %while.10 = (s32[]{:T(128)}, bf16[16,2,3,4,128,128]{4,5,3,1,2,0:T(8,128)(2,1)}, s32[16]{0:T(128)S(1)}, s32[32,4]{1,0:T(8,128)S(1)}, bf16[384,16,128]{2,0,1:T(8,1...) while((s32[]{:T(128)}, ...), condition=%wide.region_6.9_spmd, body=%wide.region_5.8_spmd.sunk | while | flops 304352384 | bytes 31798688 | solution.py:124
  520.1 2.9 gather_fusion.1
  523.0 2.5 copy.95
  537.4 2.9 gather_fusion.1
  540.4 2.5 copy.95
  554.8 2.9 gather_fusion.1
  572.2 2.9 gather_fusion.1
  589.6 2.9 gather_fusion.1
  606.9 2.9 gather_fusion.1
  624.3 2.9 gather_fusion.1
  641.7 2.9 gather_fusion.1
  659.1 2.9 gather_fusion.1
  676.4 2.9 gather_fusion.1
  693.9 2.9 gather_fusion.1
  711.2 2.9 gather_fusion.1
  728.7 2.9 gather_fusion.1
  746.1 2.9 gather_fusion.1
  763.5 2.9 gather_fusion.1
  780.8 2.9 gather_fusion.1
  796.9 16.6 %copy.69 = bf16[16,2,3,4,128,128]{5,4,3,1,0,2:T(8,128)(2,1)} copy(bf16[16,2,3,4,128,128]{4,5,3,1,2,0:T(8,128)(2,1)} %get-tuple-element.64) | data formatting | bytes 25165824 | tf_op jit(solution)/shard_map/convert_element_type | solution.py:126
  814.9 8.5 gather_fusion.5
  823.4 8.6 gather_fusion.4
  832.1 8.1 fusion.25
  840.2 8.1 fusion.37
  848.3 4.9 copy.66
  853.4 8.8 gather_fusion.3
  862.2 8.0 bitcast_convert_fusion
  870.3 3.0 copy.61
  874.5 217.0 %all-reduce.3.cloned.1.call-done = bf16[32,3,4,128,128]{4,3,2,0,1:T(8,128)(2,1)} async-done(((bf16[32,3,4,128,128]{4,3,2,0,1:T(8,128)(2,1)}), bf16[32,3,4,128,128]{4,3,2,0,1:T(8,128)(2,1)}) %all-reduce.3.cloned.1.call-update) | async-done | bytes 12582928
  1093.6 75.2 %reduce-scatter.8.cloned.1.call-done = bf16[384,512]{1,0:T(8,128)(2,1)} async-done(((bf16[384,4096]{1,0:T(8,128)(2,1)}), bf16[384,512]{1,0:T(8,128)(2,1)}) %reduce-scatter.8.cloned.1.call-update) | async-done | bytes 393232 | tf_op jit(solution)/shard_map/reduce_scatter | solution.py:88
  1168.8 74.5 %reduce-scatter.6.cloned.1.call-done = bf16[384,512]{1,0:T(8,128)(2,1)} async-done(((bf16[384,4096]{1,0:T(8,128)(2,1)}), bf16[384,512]{1,0:T(8,128)(2,1)}) %reduce-scatter.6.cloned.1.call-update) | async-done | bytes 393232 | tf_op jit(solution)/shard_map/reduce_scatter | solution.py:56
  (458 shorter events, 230.3 us)
Async XLA Ops:
  7.2 80.3 %all-gather.11.cloned.1.call-start = ((), (), s32[]{:S(2)}) async-start(), calls=%async_computation.3 | async-start | bytes 3538944 | tf_op jit(solution)/shard_map/all_gather | solution.py:22
  9.1 133.3 %all-gather.9.cloned.1.call-start = ((), (), s32[]{:S(2)}) async-start(), calls=%async_computation.2 | async-start | bytes 4456448 | tf_op jit(solution)/shard_map/all_gather | solution.py:28
  9.9 189.7 %all-gather.13.cloned.1.call-start = ((), (), s32[]{:S(2)}) async-start(), calls=%async_computation.4 | async-start | bytes 4456448 | tf_op jit(solution)/shard_map/all_gather | solution.py:29
  10.6 260.7 %all-gather.17.cloned.1.call-start = ((), (), s32[]{:S(2)}) async-start(), calls=%async_computation.7 | async-start | bytes 3538944 | tf_op jit(solution)/shard_map/all_gather | solution.py:23
  12.6 317.3 %all-gather.15.cloned.1.call-start = ((), (), s32[]{:S(2)}) async-start(), calls=%async_computation.5 | async-start | bytes 4456448 | tf_op jit(solution)/shard_map/all_gather | solution.py:46
  13.2 1078.4 %all-reduce.3.cloned.1.call-start = ((), (), s32[]{:S(2)}) async-start(), calls=%async_computation.9 | async-start | bytes 25165824
  42.0 45.3 %copy-start.11 = (s32[4,8,4]{2,1,0:T(8,128)}, s32[4,8,4]{2,1,0:T(8,128)S(1)}, u32[]{:S(2)}) copy-start(s32[4,8,4]{2,1,0:T(8,128)S(1)} %convert_subtract_fusion.2) | copy-start | bytes 1540
  62.0 95.7 %copy-start.13 = (s32[4,8,4]{2,1,0:T(8,128)}, s32[4,8,4]{2,1,0:T(8,128)S(1)}, u32[]{:S(2)}) copy-start(s32[4,8,4]{2,1,0:T(8,128)S(1)} %convert_subtract_fusion.1) | copy-start | bytes 1540
  87.2 70.4 %copy-start.9 = (s32[4,8,4]{2,1,0:T(8,128)}, s32[4,8,4]{2,1,0:T(8,128)S(1)}, u32[]{:S(2)}) copy-start(s32[4,8,4]{2,1,0:T(8,128)S(1)} %convert_subtract_fusion) | copy-start | bytes 1540
  157.7 41.9 %copy-start.6 = (bf16[384,4096]{0,1:T(8,128)(2,1)S(1)}, bf16[384,4096]{0,1:T(8,128)(2,1)}, u32[]{:S(2)}) copy-start(bf16[384,4096]{0,1:T(8,128)(2,1)} %all-gather.11.cloned.1.call-done) | copy-start | bytes 9437188
  408.6 65.3 %copy-start = (f32[384,16,128]{2,0,1:T(8,128)}, f32[384,16,128]{2,0,1:T(8,128)S(1)}, u32[]{:S(2)}) copy-start(f32[384,16,128]{2,0,1:T(8,128)S(1)} %scatter_fusion) | copy-start | bytes 9437188
  512.9 5.8 copy-start.10
  518.7 9.3 copy-start.3
  523.0 9.5 copy-start.1
  536.1 9.3 copy-start.3
  540.4 9.5 copy-start.1
  553.4 9.3 copy-start.3
  557.7 9.5 copy-start.1
  570.8 9.3 copy-start.3
  575.1 9.5 copy-start.1
  588.2 9.3 copy-start.3
  592.5 9.5 copy-start.1
  605.6 9.3 copy-start.3
  609.9 9.5 copy-start.1
  622.9 9.3 copy-start.3
  627.2 9.5 copy-start.1
  640.3 9.3 copy-start.3
  644.6 9.5 copy-start.1
  657.7 9.3 copy-start.3
  662.0 9.5 copy-start.1
  675.1 9.3 copy-start.3
  679.4 9.5 copy-start.1
  692.5 9.3 copy-start.3
  696.8 9.5 copy-start.1
  709.9 9.3 copy-start.3
  714.2 9.5 copy-start.1
  727.3 9.3 copy-start.3
  731.6 9.5 copy-start.1
  744.7 9.3 copy-start.3
  749.0 9.5 copy-start.1
  762.1 9.3 copy-start.3
  766.4 9.5 copy-start.1
  779.5 9.3 copy-start.3
  783.8 9.5 copy-start.1
  813.5 355.3 %reduce-scatter.8.cloned.1.call-start = ((), (), s32[]{:S(2)}) async-start(), calls=%async_computation.8 | async-start | bytes 3538944 | tf_op jit(solution)/shard_map/reduce_scatter | solution.py:88
  814.9 8.5 copy-start.4
  832.1 8.1 copy-start.7
  853.2 390.1 %reduce-scatter.6.cloned.1.call-start = ((), (), s32[]{:S(2)}) async-start(), calls=%async_computation.6 | async-start | bytes 3538944 | tf_op jit(solution)/shard_map/reduce_scatter | solution.py:56
  (21 other events, 107.9 us)
Sparse Core Ops, SparseCore 0:
  10.2 72.9 all-gather.10
  85.6 56.7 all-gather.8
  144.9 54.6 all-gather.12
  201.7 69.5 all-gather.16
  273.5 56.3 all-gather.14
  813.7 277.8 all-reduce.2
  1094.6 74.1 reduce-scatter.7
  1171.8 71.5 reduce-scatter.5
where the time goes:
time: 1260 us; the launch traced here: 1250 us
  waiting for transfers between devices  532 us (42%)
  local copies, waits for them, and re-layouts  302 us (24%)
  other arithmetic  167 us (13%)
  matrix products  150 us (12%)
  blocking collectives  71.7 us (6%)
  between operations  15.1 us (1%)
    unnamed x9, waiting for transfers between devices  219 us
    scatter-add x3, other arithmetic, spread_columns(): return empty.at[:, columns.reshape(-1)].add(flat)  140 us
    gather x32, local copies, waits for them, and re-layouts, one_group(): jnp.take(up_delta, up_local, axis=1)  86.3 us
    reduce_scatter x1, waiting for transfers between devices, body(): lax.psum_scatter(partial_value.reshape(tok_rows, -1).astype(jnp.bfloat16)...  75.2 us
    reduce_scatter x1, waiting for transfers between devices, body(): lax.psum_scatter(out_acc.reshape(tok_rows, -1).astype(jnp.bfloat16), 'col...  74.5 us
    reshape x3, local copies, waits for them, and re-layouts, spread_columns(): flat = products.reshape(tok_rows, -1, products.shape[3])  74.5 us
    all_gather x1, waiting for transfers between devices, body(): down_vals = lax.all_gather(down_blocks, 'row', axis=0, tiled=True)  58.6 us
    all_gather x1, waiting for transfers between devices, body(): gate_vals = lax.all_gather(gate_blocks, 'row', axis=0, tiled=True)  55 us
  transfers between devices with their start and end apart: 8, of which 7 were waited for; matrix products, arithmetic and copies ran while one was open for 12% of the time, Pallas kernels for 0%

commit v1 on v0

--- a/solution.py
+++ b/solution.py
@@ -43,7 +43,9 @@
     gate_acc, up_acc, gate_idx, up_idx = (gate_acc, up_acc, gate_gate_idx, gate_up_idx)
     silu_gate = jax.nn.silu(gate_acc)
     hidden_blocks = (silu_gate * up_acc).astype(jnp.bfloat16)
-    down_vals = lax.all_gather(down_blocks, "row", axis=0, tiled=True)
+    down_vals = jnp.concatenate(
+        lax.all_to_all(jnp.stack([down_blocks] * lax.axis_size("row")), "row", 0, 0), axis=0
+    )
     down_piece = lax.all_gather(down_cols.astype(jnp.bfloat16), "row", axis=0, tiled=True)
     down_local = down_piece.astype(jnp.int32) - offset
     chosen = jnp.take(hidden_blocks, down_local, axis=1)

time: 1260 us -> 1300 us (1.032)
  waiting for transfers between devices: 532 us -> 570 us
    all_to_all x0 -> x1, waiting for transfers between devices: none -> 54.1 us  [body(): lax.all_to_all(jnp.stack([down_blocks] * lax.axis_size('row')), 'row', 0, 0)]
    unnamed x9, waiting for transfers between devices: 219 us -> 203 us
  transfers between devices with their start and end apart: 8 -> 9, of which waited for: 7 -> 8; matrix products, arithmetic and copies ran while one was open for 12% -> 11% of each run, Pallas kernels for 0% -> 0%
where the time goes in v1:
time: 1300 us
  waiting for transfers between devices  570 us (44%)
  local copies, waits for them, and re-layouts  303 us (23%)
  other arithmetic  167 us (13%)
  matrix products  152 us (12%)
  blocking collectives  71.7 us (6%)
  between operations  15.1 us (1%)
    unnamed x9, waiting for transfers between devices  203 us
    scatter-add x3, other arithmetic, spread_columns(): return empty.at[:, columns.reshape(-1)].add(flat)  141 us
    gather x32, local copies, waits for them, and re-layouts, one_group(): jnp.take(up_delta, up_local, axis=1)  86.5 us
    reduce_scatter x1, waiting for transfers between devices, body(): lax.psum_scatter(partial_value.reshape(tok_rows, -1).astype(jnp.bfloat16)...  75.2 us
    reduce_scatter x1, waiting for transfers between devices, body(): lax.psum_scatter(out_acc.reshape(tok_rows, -1).astype(jnp.bfloat16), 'col...  74.5 us
    reshape x3, local copies, waits for them, and re-layouts, spread_columns(): flat = products.reshape(tok_rows, -1, products.shape[3])  74.5 us
    all_gather x1, waiting for transfers between devices, body(): lax.all_gather(down_blocks, 'row', axis=0, tiled=True)  58.6 us
    all_gather x1, waiting for transfers between devices, body(): gate_vals = lax.all_gather(gate_blocks, 'row', axis=0, tiled=True)  55 us
  transfers between devices with their start and end apart: 9, of which 8 were waited for; matrix products, arithmetic and copies ran while one was open for 11% of the time, Pallas kernels for 0%

profile of v1, /device:TPU:2, one launch (start us, length us, event | category | flops | bytes accessed | tf_op | source)
XLA Modules:
  0.0 1296.0 jit_solution(18024815520208544493)
XLA Ops:
  14.0 28.0 %all-gather = bf16[16,2,4]{2,1,0:T(2,128)(2,1)S(1)} all-gather(bf16[1,2,4]{2,1,0:T(2,128)(2,1)S(1)} %convert_bitcast_fusion.2), channel_id=1, replica_groups=mesh['row'=16,'col'=8] {'row'}, dimensions={0}, use_global_device_ids=true | all-gather | bytes 272 | tf_op jit(solution)/shard_map/all_gather | solution.py:30
  42.8 19.2 %all-gather.1 = bf16[16,2,4]{2,1,0:T(2,128)(2,1)S(1)} all-gather(bf16[1,2,4]{2,1,0:T(2,128)(2,1)S(1)} %convert_bitcast_fusion.1), channel_id=1, replica_groups=mesh['row'=16,'col'=8] {'row'}, dimensions={0}, use_global_device_ids=true | all-gather | bytes 272 | tf_op jit(solution)/shard_map/all_gather | solution.py:31
  62.8 24.5 %all-gather.2 = bf16[16,2,4]{2,1,0:T(2,128)(2,1)S(1)} all-gather(bf16[1,2,4]{2,1,0:T(2,128)(2,1)S(1)} %convert_bitcast_fusion), channel_id=1, replica_groups=mesh['row'=16,'col'=8] {'row'}, dimensions={0}, use_global_device_ids=true | all-gather | bytes 272 | tf_op jit(solution)/shard_map/all_gather | solution.py:49
  87.4 55.0 %all-gather.9.cloned.1.call-done = bf16[32,4,128,128]{3,2,1,0:T(8,128)(2,1)} async-done(((bf16[2,4,128,128]{3,2,1,0:T(8,128)(2,1)}), bf16[32,4,128,128]{3,2,1,0:T(8,128)(2,1)}) %all-gather.9.cloned.1.call-update) | async-done | bytes 4194320 | tf_op jit(solution)/shard_map/all_gather | solution.py:28
  142.5 15.2 %fusion.52 = f32[32,4,128,384]{3,2,1,0:T(8,128)} fusion(bf16[32,4,128,128]{3,2,1,0:T(8,128)(2,1)} %all-gather.9.cloned.1.call-done, bf16[384,32,128,1]{0,2,3,1:T(8,128)(2,1)} %bitcast.177), kind=kOutput, calls=%fused_computation.100 | convolution fusion | flops 1610612736 | bytes 32505856 | tf_op jit(solution)/shard_map/tkd,kjde->tkje/dot_general | solution.py:35
  157.7 25.0 %copy.57 = f32[384,128,128]{2,0,1:T(8,128)} copy(f32[384,128,128]{0,2,1:T(8,128)} %bitcast.168) | data formatting | bytes 50331648 | tf_op jit(solution)/shard_map/reshape | solution.py:9
  182.7 16.9 %all-gather.13.cloned.1.call-done = bf16[32,4,128,128]{3,2,1,0:T(8,128)(2,1)} async-done(((bf16[2,4,128,128]{3,2,1,0:T(8,128)(2,1)}), bf16[32,4,128,128]{3,2,1,0:T(8,128)(2,1)}) %all-gather.13.cloned.1.call-update) | async-done | bytes 4194320 | tf_op jit(solution)/shard_map/all_gather | solution.py:29
  199.6 14.1 %fusion.53 = f32[32,4,128,384]{3,2,1,0:T(8,128)} fusion(bf16[32,4,128,128]{3,2,1,0:T(8,128)(2,1)} %all-gather.13.cloned.1.call-done, bf16[384,32,128,1]{0,2,3,1:T(8,128)(2,1)S(1)} %bitcast.179), kind=kOutput, calls=%fused_computation.101 | convolution fusion | flops 1610612736 | bytes 32505856 | tf_op jit(solution)/shard_map/tkd,kjde->tkje/dot_general | solution.py:38
  213.7 24.8 %copy.60 = f32[384,128,128]{2,0,1:T(8,128)} copy(f32[384,128,128]{0,2,1:T(8,128)} %bitcast.169) | data formatting | bytes 50331648 | tf_op jit(solution)/shard_map/reshape | solution.py:9
  238.5 32.8 %all-gather.17.cloned.1.call-done = bf16[384,4096]{0,1:T(8,128)(2,1)} async-done(((bf16[384,512]{0,1:T(8,128)(2,1)}), bf16[384,4096]{0,1:T(8,128)(2,1)}) %all-gather.17.cloned.1.call-update) | async-done | bytes 3145744 | tf_op jit(solution)/shard_map/all_gather | solution.py:23
  271.3 58.6 %all-gather.15.cloned.1.call-done = bf16[32,4,128,128]{3,2,1,0:T(8,128)(2,1)} async-done(((bf16[2,4,128,128]{3,2,1,0:T(8,128)(2,1)}), bf16[32,4,128,128]{3,2,1,0:T(8,128)(2,1)}) %all-gather.15.cloned.1.call-update) | async-done | bytes 4194320 | tf_op jit(solution)/shard_map/all_gather | solution.py:65
  329.9 15.0 %fusion.54 = f32[32,4,128,384]{3,2,1,0:T(8,128)} fusion(bf16[32,4,128,128]{3,2,1,0:T(8,128)(2,1)} %all-gather.15.cloned.1.call-done, bf16[384,32,128,1]{0,2,3,1:T(8,128)(2,1)} %bitcast.183), kind=kOutput, calls=%fused_computation.102 | convolution fusion | flops 1610612736 | bytes 32505856 | tf_op jit(solution)/shard_map/tkd,kjde->tkje/dot_general | solution.py:62
  344.9 24.7 %copy.65 = f32[384,128,128]{2,0,1:T(8,128)} copy(f32[384,128,128]{0,2,1:T(8,128)} %bitcast.167) | data formatting | bytes 50331648 | tf_op jit(solution)/shard_map/reshape | solution.py:9
  369.9 38.7 %scatter_fusion = f32[384,16,128]{2,0,1:T(8,128)S(1)} fusion(f32[384,16,128]{2,0,1:T(8,128)S(1)} %broadcast.82.clone, s32[128]{0:T(128)S(1)} %fusion.46, f32[128,384,128]{2,1,0:T(8,128)} %bitcast.170), kind=kCustom, calls=%fused_computation.6 | custom fusion | flops 6291456 | bytes 75497984 | tf_op jit(solution)/shard_map/scatter-add | solution.py:11
  410.8 63.2 %scatter_fusion.1 = f32[384,16,128]{2,0,1:T(8,128)} fusion(f32[384,16,128]{2,0,1:T(8,128)} %broadcast.82.clone.2, s32[128]{0:T(128)S(1)} %fusion.47, f32[128,384,128]{2,1,0:T(8,128)} %bitcast.171), kind=kCustom, calls=%fused_computation.7 | custom fusion | flops 6291456 | bytes 75497984 | tf_op jit(solution)/shard_map/scatter-add | solution.py:11
  474.3 38.7 %scatter_fusion.2 = f32[384,16,128]{2,0,1:T(8,128)S(1)} fusion(f32[384,16,128]{2,0,1:T(8,128)S(1)} %broadcast.82.clone.1, s32[128]{0:T(128)S(1)} %fusion.48, f32[128,384,128]{2,1,0:T(8,128)} %bitcast.172), kind=kCustom, calls=%fused_computation.8 | custom fusion | flops 6291456 | bytes 75497984 | tf_op jit(solution)/shard_map/scatter-add | solution.py:11
  513.1 5.7 multiply_convert_fusion.1
  518.8 278.3 %while.10 = (s32[]{:T(128)}, bf16[16,2,3,4,128,128]{4,5,3,1,2,0:T(8,128)(2,1)}, s32[16]{0:T(128)S(1)}, s32[32,4]{1,0:T(8,128)S(1)}, bf16[384,16,128]{2,0,1:T(8,1...) while((s32[]{:T(128)}, ...), condition=%wide.region_6.9_spmd, body=%wide.region_5.8_spmd.sunk | while | flops 304352384 | bytes 31798688 | solution.py:126
  520.2 3.0 gather_fusion.1
  537.6 3.0 gather_fusion.1
  554.9 3.0 gather_fusion.1
  572.4 3.0 gather_fusion.1
  589.7 3.0 gather_fusion.1
  607.1 3.0 gather_fusion.1
  624.5 3.0 gather_fusion.1
  641.9 3.0 gather_fusion.1
  659.3 3.0 gather_fusion.1
  676.6 3.0 gather_fusion.1
  694.1 3.0 gather_fusion.1
  711.5 3.0 gather_fusion.1
  728.9 3.0 gather_fusion.1
  746.3 3.0 gather_fusion.1
  763.7 3.0 gather_fusion.1
  781.1 3.0 gather_fusion.1
  797.1 16.6 %copy.69 = bf16[16,2,3,4,128,128]{5,4,3,1,0,2:T(8,128)(2,1)} copy(bf16[16,2,3,4,128,128]{4,5,3,1,2,0:T(8,128)(2,1)} %get-tuple-element.64) | data formatting | bytes 25165824 | tf_op jit(solution)/shard_map/convert_element_type | solution.py:128
  815.2 8.6 gather_fusion.5
  823.8 8.5 gather_fusion.4
  832.3 9.7 fusion.25
  842.1 8.8 fusion.37
  850.9 3.0 copy.66
  854.0 3.0 stack.10
  857.0 4.7 all-to-all-start
  861.9 8.5 gather_fusion.3
  870.4 54.1 %all-to-all-done = bf16[16,2,4,128,128]{4,3,2,1,0:T(8,128)(2,1)} async-done(((bf16[16,2,4,128,128]{4,3,2,1,0:T(8,128)(2,1)}), bf16[16,2,4,128,128]{4,3,2,1,0:T(8,128)(2,1)}, u32[]{:S(2)}, u32[]{:S(2)}) %all-to-all-start) | async-done | bytes 4194336 | tf_op jit(solution)/shard_map/all_to_all | solution.py:47
  924.5 8.0 bitcast_convert_fusion
  936.8 200.6 %all-reduce.3.cloned.1.call-done = bf16[32,3,4,128,128]{4,3,2,0,1:T(8,128)(2,1)} async-done(((bf16[32,3,4,128,128]{4,3,2,0,1:T(8,128)(2,1)}), bf16[32,3,4,128,128]{4,3,2,0,1:T(8,128)(2,1)}) %all-reduce.3.cloned.1.call-update) | async-done | bytes 12582928
  1139.4 75.2 %reduce-scatter.8.cloned.1.call-done = bf16[384,512]{1,0:T(8,128)(2,1)} async-done(((bf16[384,4096]{1,0:T(8,128)(2,1)}), bf16[384,512]{1,0:T(8,128)(2,1)}) %reduce-scatter.8.cloned.1.call-update) | async-done | bytes 393232 | tf_op jit(solution)/shard_map/reduce_scatter | solution.py:90
  1214.6 74.5 %reduce-scatter.6.cloned.1.call-done = bf16[384,512]{1,0:T(8,128)(2,1)} async-done(((bf16[384,4096]{1,0:T(8,128)(2,1)}), bf16[384,512]{1,0:T(8,128)(2,1)}) %reduce-scatter.6.cloned.1.call-update) | async-done | bytes 393232 | tf_op jit(solution)/shard_map/reduce_scatter | solution.py:58
  (463 shorter events, 237.9 us)
Async XLA Ops:
  7.2 80.3 %all-gather.11.cloned.1.call-start = ((), (), s32[]{:S(2)}) async-start(), calls=%async_computation.4 | async-start | bytes 3538944 | tf_op jit(solution)/shard_map/all_gather | solution.py:22
  9.1 133.3 %all-gather.9.cloned.1.call-start = ((), (), s32[]{:S(2)}) async-start(), calls=%async_computation.3 | async-start | bytes 4456448 | tf_op jit(solution)/shard_map/all_gather | solution.py:28
  9.9 189.7 %all-gather.13.cloned.1.call-start = ((), (), s32[]{:S(2)}) async-start(), calls=%async_computation.5 | async-start | bytes 4456448 | tf_op jit(solution)/shard_map/all_gather | solution.py:29
  10.6 260.7 %all-gather.17.cloned.1.call-start = ((), (), s32[]{:S(2)}) async-start(), calls=%async_computation.8 | async-start | bytes 3538944 | tf_op jit(solution)/shard_map/all_gather | solution.py:23
  12.6 317.3 %all-gather.15.cloned.1.call-start = ((), (), s32[]{:S(2)}) async-start(), calls=%async_computation.7 | async-start | bytes 4456448 | tf_op jit(solution)/shard_map/all_gather | solution.py:65
  13.2 1124.2 %all-reduce.3.cloned.1.call-start = ((), (), s32[]{:S(2)}) async-start(), calls=%async_computation.10 | async-start | bytes 25165824
  42.0 45.3 %copy-start.12 = (s32[4,8,4]{2,1,0:T(8,128)}, s32[4,8,4]{2,1,0:T(8,128)S(1)}, u32[]{:S(2)}) copy-start(s32[4,8,4]{2,1,0:T(8,128)S(1)} %convert_subtract_fusion.2) | copy-start | bytes 1540
  62.0 95.7 %copy-start.14 = (s32[4,8,4]{2,1,0:T(8,128)}, s32[4,8,4]{2,1,0:T(8,128)S(1)}, u32[]{:S(2)}) copy-start(s32[4,8,4]{2,1,0:T(8,128)S(1)} %convert_subtract_fusion.1) | copy-start | bytes 1540
  87.2 70.4 %copy-start.10 = (s32[4,8,4]{2,1,0:T(8,128)}, s32[4,8,4]{2,1,0:T(8,128)S(1)}, u32[]{:S(2)}) copy-start(s32[4,8,4]{2,1,0:T(8,128)S(1)} %convert_subtract_fusion) | copy-start | bytes 1540
  157.7 41.9 %copy-start.6 = (bf16[384,4096]{0,1:T(8,128)(2,1)S(1)}, bf16[384,4096]{0,1:T(8,128)(2,1)}, u32[]{:S(2)}) copy-start(bf16[384,4096]{0,1:T(8,128)(2,1)} %all-gather.11.cloned.1.call-done) | copy-start | bytes 9437188
  408.6 65.5 %copy-start = (f32[384,16,128]{2,0,1:T(8,128)}, f32[384,16,128]{2,0,1:T(8,128)S(1)}, u32[]{:S(2)}) copy-start(f32[384,16,128]{2,0,1:T(8,128)S(1)} %scatter_fusion) | copy-start | bytes 9437188
  518.8 9.3 copy-start.3
  523.1 9.5 copy-start.1
  536.2 9.3 copy-start.3
  540.5 9.5 copy-start.1
  553.6 9.3 copy-start.3
  557.9 9.5 copy-start.1
  571.0 9.3 copy-start.3
  575.4 9.5 copy-start.1
  588.4 9.3 copy-start.3
  592.7 9.5 copy-start.1
  605.8 9.3 copy-start.3
  610.1 9.5 copy-start.1
  623.1 9.3 copy-start.3
  627.5 9.5 copy-start.1
  640.5 9.3 copy-start.3
  644.9 9.5 copy-start.1
  657.9 9.3 copy-start.3
  662.2 9.5 copy-start.1
  675.3 9.3 copy-start.3
  679.6 9.5 copy-start.1
  692.7 9.3 copy-start.3
  697.0 9.5 copy-start.1
  710.1 9.3 copy-start.3
  714.4 9.5 copy-start.1
  727.5 9.3 copy-start.3
  731.8 9.5 copy-start.1
  744.9 9.3 copy-start.3
  749.2 9.5 copy-start.1
  762.3 9.3 copy-start.3
  766.7 9.5 copy-start.1
  779.8 9.3 copy-start.3
  784.1 9.5 copy-start.1
  813.8 400.8 %reduce-scatter.8.cloned.1.call-start = ((), (), s32[]{:S(2)}) async-start(), calls=%async_computation.9 | async-start | bytes 3538944 | tf_op jit(solution)/shard_map/reduce_scatter | solution.py:90
  815.2 8.6 copy-start.4
  832.3 9.7 copy-start.7
  857.0 67.5 %all-to-all-start = ((bf16[16,2,4,128,128]{4,3,2,1,0:T(8,128)(2,1)}), bf16[16,2,4,128,128]{4,3,2,1,0:T(8,128)(2,1)}, u32[]{:S(2)}, u32[]{:S(2)}) async-start(bf16[16,2,4,128,128]{4,3,2,1,0:T(8,128)(2,1)} %stack.10), calls=%async_computation | async-start | bytes 8388608 | tf_op jit(solution)/shard_map/all_to_all | solution.py:47
  861.7 427.5 %reduce-scatter.6.cloned.1.call-start = ((), (), s32[]{:S(2)}) async-start(), calls=%async_computation.6 | async-start | bytes 3538944 | tf_op jit(solution)/shard_map/reduce_scatter | solution.py:58
  (23 other events, 116.3 us)
Sparse Core Ops, SparseCore 0:
  10.2 72.9 all-gather.10
  85.6 56.7 all-gather.8
  144.9 54.6 all-gather.12
  201.7 69.5 all-gather.16
  273.5 56.3 all-gather.14
  813.9 323.4 all-reduce.2
  1140.4 74.1 reduce-scatter.7
  1217.6 71.5 reduce-scatter.5
